TPU v7x, 128 devices: a whole 4x4x4 slice. The times are simulated.
128 devices in a mesh: exa: 8 (over z, core), exb: 16 (over x, y).
Axes of the slice: x: 4, y: 4, z: 4, core: 2. Of those that a mesh axis runs over, the one named last changes fastest.
Arguments:
- features: float32 [1048576, 128], P(('exa', 'exb')), may hold values from -6 to 6
- sign_bits: int32 [1048576], P(('exa', 'exb')), may hold values from 0 to 1
- sample_device: int32 [65536, 1], replicated, may hold values from 0 to 127; in each aligned block of 512 rows (0 to 511, 512 to 1023, ...) at most 8 rows name the same one
- sample_offset: int32 [65536], replicated, may hold values from 0 to 8191, as said below
Outputs:
- q_rows: float32 [65536, 128], P(('exa', 'exb'))
- upper_factor: float32 [128, 128], replicated
Inputs may be any that keep to these rules, and one draw needn't show every extreme that they name: `sample_device`: within each aligned block of 512 rows no value appears more than 8 times. `sample_offset`: within each aligned block of 512 rows, at most 8 values fall into any one range of 64 consecutive offsets that starts at a multiple of 64, and in every block some range holds exactly 8.
All inputs are finite; a program needn't handle non-finite values.
Results may differ from a plain program's by a relative error of at most 0.000071.
Values sent between devices are 32-bit elements; how exact they have to be, the bound alone decides.
A program may use at most 64 MiB of HBM per device.

v0:
```python
import jax
import jax.numpy as jnp
from jax import lax
from jax.experimental import pallas as pl
from jax.experimental.pallas import tpu as pltpu
from jax.sharding import PartitionSpec as P

MESH = pl.DeviceIdType.MESH
GROUP_BITS = (6, 5, 3, 2, 1, 0)
STEPS = (96, 32, 12, 4, 3, 1)
CORE_BIT = 4
FIRST = (5, 0, 1, 3, 4, 2, 3, 4, 5, 5, 0, 2, 1, 1, 1, 0)
ORDER = (
    (0, 0), (1, 0), (2, 0), (3, 0), (4, 0), (5, 0), (6, 0), (7, 0), (0, 1), (1, 1),
    (2, 1), (3, 1), (4, 1), (5, 1), (8, 1), (10, 1), (12, 1), (6, 1), (7, 1), (11, 1),
    (9, 1), (15, 1), (13, 1), (5, 2), (3, 2), (2, 2), (4, 2), (0, 2), (14, 1), (11, 2),
    (6, 2), (12, 2), (7, 2), (8, 2), (1, 2), (2, 3), (5, 3), (13, 2), (3, 3), (9, 2),
    (10, 2), (12, 3), (11, 3), (14, 2), (6, 3), (4, 3), (15, 2), (13, 3), (2, 4), (1, 3),
    (5, 4), (7, 3), (0, 3), (14, 3), (12, 4), (10, 3), (11, 4), (3, 4), (8, 3), (1, 4),
    (13, 4), (15, 3), (2, 5), (6, 4), (9, 3), (10, 4), (14, 4), (0, 4), (12, 5), (5, 5),
    (4, 4), (15, 4), (1, 5), (8, 4), (13, 5), (11, 5), (7, 4), (0, 5), (10, 5), (9, 4),
    (14, 5), (2, 6), (3, 5), (8, 5), (15, 5), (4, 5), (1, 6), (12, 6), (6, 5), (9, 5),
    (0, 6), (7, 5), (10, 6), (13, 6), (5, 6), (4, 6), (8, 6), (3, 6), (15, 6), (14, 6),
    (11, 6), (7, 6), (9, 6), (6, 6),
)
SCALE = 1.0 / 1024.0


def bit_of(number, bit):
    return (number // (1 << bit)) % 2


def flip(number, mask):
    for bit in range(7):
        if mask >> bit & 1:
            number = number + (1 << bit) * (1 - 2 * bit_of(number, bit))
    return number


def group_of(device):
    out = 0
    for bit in range(7):
        value = bit_of(device, bit)
        if bit in (0, 2, 5):
            above = bit_of(device, bit + 1)
            value = value + above - 2 * value * above
        out = out + value * (1 << bit)
    return out


def place_of(device):
    return (device // 16, device % 16)


def sublane_hadamard(tile, rows):
    for step in (4, 2, 1):
        high = (rows // step) % 2 == 1
        if step == 4:
            other = pltpu.roll(tile, 4, 0)
        else:
            other = jnp.where(high, pltpu.roll(tile, step, 0), pltpu.roll(tile, 8 - step, 0))
        tile = jnp.where(high, other - tile, tile + other)
    return tile


def factor(gram, upper_ref, inverse_ref, work, beside):
    width, size = 128, 16
    rows = lax.broadcasted_iota(jnp.int32, (8, width), 0)
    lanes = lax.broadcasted_iota(jnp.int32, (8, width), 1)
    work[:, :width] = gram
    work[:, width:] = (
        lax.broadcasted_iota(jnp.int32, (width, width), 0)
        == lax.broadcasted_iota(jnp.int32, (width, width), 1)
    ).astype(jnp.float32)
    both = work[:size, :]
    for panel in range(width // size):
        beside(panel)
        low, end = size * panel, size * (panel + 1)
        left = [both[8 * t : 8 * t + 8, :width] for t in range(2)]
        right = [both[8 * t : 8 * t + 8, width:] for t in range(2)]
        cols = [
            [jnp.broadcast_to(tile[:, low + j : low + j + 1], (8, width)) for tile in left]
            for j in range(size)
        ]
        pivots = [jnp.ones((8, width), jnp.float32) for _ in range(2)]
        for i in range(size):
            own, row = divmod(i, 8)
            pivot = jnp.broadcast_to(cols[i][own][row : row + 1, :], (8, width))
            pivots[own] = jnp.where(rows == row, pivot, pivots[own])
            left_row, right_row = left[own][row : row + 1, :], right[own][row : row + 1, :]
            col_row = [cols[j][own][row : row + 1, :] for j in range(size)]
            for t in range(own, 2):
                if t == own and row == 7:
                    continue
                scaled = cols[i][t] / pivot
                if t == own:
                    scaled = jnp.where(rows > row, scaled, 0.0)
                for j in range(i + 1, size):
                    cols[j][t] = cols[j][t] - scaled * col_row[j]
                left[t] = left[t] - scaled * left_row
                right[t] = right[t] - scaled * right_row
        for t in range(2):
            root = lax.rsqrt(pivots[t])
            root = root * (1.5 - 0.5 * pivots[t] * root * root)
            left[t] = jnp.where(lanes >= rows + (low + 8 * t), left[t] * root, 0.0)
            right[t] = right[t] * root
            upper_ref[low + 8 * t : low + 8 * t + 8, :] = left[t]
            inverse_ref[low + 8 * t : low + 8 * t + 8, :] = right[t]
        if end < width:
            top = jnp.concatenate(left, axis=0)
            turned = top.T
            top = jnp.concatenate([top, jnp.concatenate(right, axis=0)], axis=1)
            both = work[end : end + size, :] - dot_exact(turned[end : end + size, :], top, ((1,), (0,)))
            if end + size < width:
                work[end + size :, :] = work[end + size :, :] - dot_exact(
                    turned[end + size :, :], top, ((1,), (0,))
                )


def dot_exact(a, b, contract):
    return lax.dot_general(
        a,
        b,
        (contract, ((), ())),
        precision=lax.Precision.HIGHEST,
        preferred_element_type=jnp.float32,
    )


def sample_tables(group, device, device_ref, offset_ref, give_ref, take_ref):
    shape = (512, 128)
    offsets = offset_ref[...]
    sources = device_ref[...]
    here = offsets // 64 == group
    mine = jnp.where(here, 1.0, 0.0)
    square = (128, 128)
    first = lax.broadcasted_iota(jnp.int32, square, 0)
    second = lax.broadcasted_iota(jnp.int32, square, 1)
    before = jnp.where(first < second, 1.0, 0.0).astype(jnp.bfloat16)
    ones = jnp.ones(square, jnp.bfloat16)

    def plain(a, b):
        return lax.dot_general(
            a.astype(jnp.bfloat16),
            b.astype(jnp.bfloat16),
            (((1,), (0,)), ((), ())),
            preferred_element_type=jnp.float32,
        )

    wide = (512, 512)
    later = lax.broadcasted_iota(jnp.int32, wide, 0)
    earlier = lax.broadcasted_iota(jnp.int32, wide, 1)
    lines = jnp.where((later // 4 == earlier // 4) & (earlier < later), 1.0, 0.0)
    rank = plain(mine, before) + plain(lines, plain(mine, ones))
    value = (sources * 8192 + offsets + 1).astype(jnp.float32)
    lanes = lax.broadcasted_iota(jnp.int32, shape, 1)
    found = jnp.zeros(shape, jnp.float32)
    for k in range(8):
        chosen = jnp.where(here & (rank == float(k)), value, 0.0)
        found = jnp.where(lanes == k, jnp.sum(chosen, axis=1, keepdims=True), found)
    blocks = jnp.where(
        lax.broadcasted_iota(jnp.int32, shape, 0) // 4
        == lax.broadcasted_iota(jnp.int32, shape, 1),
        1.0,
        0.0,
    )
    slots = dot_exact(found, blocks, ((0,), (0,)))[0:8, :].astype(jnp.int32)
    full = slots - 1
    source = full // 8192
    offset = full % 8192
    natural = jnp.zeros_like(full)
    for link in range(6):
        step = STEPS[link]
        sign = jnp.zeros_like(full)
        for bit in range(7):
            if step >> bit & 1:
                sign = sign + (source // (1 << bit)) % 2
        natural = natural + (sign % 2) * (1 << (5 - link))
    part = 2 * ((offset // 8) % 8) + (source // (1 << CORE_BIT)) % 2
    spot = jnp.zeros_like(full)
    for number in range(16):
        turn = FIRST[number]
        turned = (natural % (1 << (6 - turn))) * (1 << turn) + natural // (1 << (6 - turn))
        spot = jnp.where(part == number, turned, spot)
    row = part * 512 + spot * 8 + offset % 8
    give_ref[...] = jnp.clip(jnp.where(slots > 0, row, 8192), 0, 8192)

    total = jnp.zeros(square, jnp.float32)
    for q in range(4):
        groups = offset_ref[pl.ds(4 * device + q, 1), :] // 64
        same = jnp.where(groups == first, 1.0, 0.0)
        count = plain(same, before) + total
        place = jnp.sum(same * count, axis=0, keepdims=True)
        take_ref[q : q + 1, :] = jnp.clip(groups * 8 + place.astype(jnp.int32), 0, 1023)
        total = total + plain(same, ones)


def kernel(
    features_ref,
    bits_hbm,
    device_hbm,
    offset_hbm,
    sketch,
    inverse,
    upper_ref,
    bits_ref,
    device_ref,
    offset_ref,
    rows_in,
    signs,
    core_send,
    core_keep,
    core_got,
    send,
    keep,
    got,
    held,
    give_v,
    take_v,
    give,
    take,
    outgoing,
    received,
    gram_part,
    gram_got,
    gram_row,
    gram,
    work,
    in_sem,
    table_sem,
    core_send_sem,
    core_got_sem,
    send_sem,
    got_sem,
    row_sem,
    sum_sem,
):
    device = lax.axis_index("exa") * 16 + lax.axis_index("exb")
    group = group_of(device)
    partners = [flip(device, 1 << CORE_BIT)] + [flip(device, step) for step in STEPS]
    core_sign = (1 - 2 * bit_of(group, CORE_BIT)).astype(jnp.float32)
    link_sign = [(1 - 2 * bit_of(group, bit)).astype(jnp.float32) for bit in GROUP_BITS]

    loads = [
        pltpu.make_async_copy(
            features_ref.at[pl.ds(1024 * c, 1024)], rows_in.at[pl.ds(1024 * c, 1024)], in_sem.at[c]
        )
        for c in range(8)
    ]
    small = [
        pltpu.make_async_copy(bits_hbm, bits_ref, in_sem.at[8]),
        pltpu.make_async_copy(device_hbm, device_ref, in_sem.at[9]),
        pltpu.make_async_copy(offset_hbm, offset_ref, in_sem.at[10]),
    ]
    small[0].start()
    for load in loads:
        load.start()
    small[1].start()
    small[2].start()
    barrier = pltpu.get_barrier_semaphore()
    for partner in partners:
        pl.semaphore_signal(barrier, inc=1, device_id=place_of(partner), device_id_type=MESH)

    small[0].wait()
    bits = (2 * bits_ref[...] - 1).astype(jnp.float32)
    signs[...] = jnp.transpose(jnp.concatenate([bits, bits], axis=0))

    def first_pass(pair):
        def body(low, carry):
            turned = signs[...]
            for half in range(2):
                tiles = []
                for side in range(2):
                    base = pl.multiple_of(2048 * pair + 1024 * side + 128 * low + 64 * half, 64)
                    column = 0
                    some = []
                    for t in range(8):
                        sign = jnp.broadcast_to(
                            turned[64 * half + 8 * t : 64 * half + 8 * t + 8, 8 * side : 8 * side + 1], (8, 128)
                        )
                        some.append(rows_in[pl.ds(pl.multiple_of(base + 8 * t, 8), 8), :] * sign)
                    for step in (1, 2, 4):
                        for t in range(8):
                            if not t & step:
                                a, b = some[t], some[t + step]
                                some[t], some[t + step] = a + b, a - b
                    tiles.append(some)
                spot = 16 * pair + 2 * low + half
                for t in range(8):
                    a, b = tiles[0][t], core_sign * tiles[1][t]
                    core_keep[t, spot] = a + b
                    core_send[t, spot] = a - b
            signs[...] = pltpu.roll(turned, 127, 1)
            return carry

        lax.fori_loop(0, 8, body, 0)

    def core_copy(part):
        return pltpu.make_async_remote_copy(
            src_ref=core_send.at[part],
            dst_ref=core_got.at[part],
            send_sem=core_send_sem.at[part],
            recv_sem=core_got_sem.at[part],
            device_id=place_of(partners[0]),
            device_id_type=MESH,
        )

    for pair in range(4):
        loads[2 * pair].wait()
        loads[2 * pair + 1].wait()
        first_pass(pair)
        if pair < 3:
            signs[...] = pltpu.roll(signs[...], 120, 1)
    pl.semaphore_wait(barrier, 7)
    for part in range(8):
        core_copy(part).start()

    def link_copy(part, stage):
        link = (FIRST[part] + stage - 1) % 6
        return pltpu.make_async_remote_copy(
            src_ref=send.at[part, stage - 1],
            dst_ref=got.at[part, stage - 1],
            send_sem=send_sem.at[part, stage - 1],
            recv_sem=got_sem.at[part, stage - 1],
            device_id=place_of(partners[1 + link]),
            device_id_type=MESH,
        )

    small[1].wait()
    small[2].wait()
    sample_tables(group, device, device_ref, offset_ref, give_v, take_v)
    give_copy = pltpu.make_async_copy(give_v, give, table_sem.at[0])
    take_copy = pltpu.make_async_copy(take_v, take, table_sem.at[1])
    give_copy.start()
    take_copy.start()
    give_copy.wait()
    take_copy.wait()

    lines = lax.broadcasted_iota(jnp.int32, (8, 128), 0)

    def core_stage(part, side):
        number = 2 * part + side
        turn = FIRST[number]
        sign = link_sign[turn]

        def one(rot):
            spot = rot // (1 << turn) + (rot % (1 << turn)) * (1 << (6 - turn))
            a, b = core_keep[part, spot], core_got[part, spot]
            return a + b if side == 0 else core_sign * (a - b)

        def body(step, carry):
            for more in range(4):
                j = 4 * step + more
                a, b = one(j), sign * one(j + 32)
                keep[number, 0, j] = a + b
                send[number, 0, j] = a - b
            return carry

        lax.fori_loop(0, 8, body, 0)

    def link_stage(part, stage):
        link = (FIRST[part] + stage - 1) % 6
        sign, after = link_sign[link], link_sign[(link + 1) % 6]
        old, new = (stage - 1) % 2, stage % 2

        def pair(i):
            a, b = keep[part, old, i], got[part, stage - 1, i]
            return a + b, sign * (a - b)

        def body(step, carry):
            for more in range(4):
                i = 4 * step + more
                for side, (a, b) in enumerate(zip(pair(i), pair(i + 16))):
                    if stage == 2:
                        a, b = sublane_hadamard(a, lines), sublane_hadamard(b, lines)
                    b = after * b
                    keep[part, new, 2 * i + side] = a + b
                    send[part, stage, 2 * i + side] = a - b
            return carry

        lax.fori_loop(0, 4, body, 0)

    def last_stage(part):
        sign = link_sign[(FIRST[part] + 5) % 6] * SCALE

        def body(step, carry):
            for more in range(4):
                i = 4 * step + more
                a, b = keep[part, 1, i], got[part, 5, i]
                base = pl.multiple_of(512 * part + 16 * i, 16)
                held[pl.ds(base, 8), :] = SCALE * (a + b)
                held[pl.ds(pl.multiple_of(base + 8, 8), 8), :] = sign * (a - b)
            return carry

        lax.fori_loop(0, 8, body, 0)

    for part, stage in ORDER:
        if stage == 0:
            core_copy(part).wait_recv()
            for side in range(2):
                core_stage(part, side)
                link_copy(2 * part + side, 1).start()
        else:
            link_copy(part, stage).wait_recv()
            if stage < 6:
                link_stage(part, stage)
                link_copy(part, stage + 1).start()
            else:
                last_stage(part)
    held[8192:8200, :] = jnp.zeros((8, 128), jnp.float32)

    def gather(step, carry):
        for more in range(4):
            to = 4 * step + more
            for k in range(8):
                row = jnp.clip(give[k, to], 0, 8192)
                outgoing[pl.ds(8 * to + k, 1), :] = held[pl.ds(row, 1), :]
        return carry

    lax.fori_loop(0, 32, gather, 0)

    def row_copy(to):
        return pltpu.make_async_remote_copy(
            src_ref=outgoing.at[pl.ds(pl.multiple_of(8 * to, 8), 8)],
            dst_ref=received.at[pl.ds(pl.multiple_of(8 * group, 8), 8)],
            send_sem=row_sem.at[0],
            recv_sem=row_sem.at[1],
            device_id=place_of(to),
            device_id_type=MESH,
        )

    gram_part[...] = dot_exact(outgoing[...], outgoing[...], ((0,), (0,)))

    def part_copy(to):
        return pltpu.make_async_remote_copy(
            src_ref=gram_part.at[pl.ds(to, 1)],
            dst_ref=gram_got.at[pl.ds(device, 1)],
            send_sem=sum_sem.at[0],
            recv_sem=sum_sem.at[1],
            device_id=place_of(to),
            device_id_type=MESH,
        )

    def sum_copy(to):
        return pltpu.make_async_remote_copy(
            src_ref=gram_row,
            dst_ref=gram.at[pl.ds(device, 1)],
            send_sem=sum_sem.at[2],
            recv_sem=sum_sem.at[3],
            device_id=place_of(to),
            device_id_type=MESH,
        )

    exa, exb = lax.axis_index("exa"), lax.axis_index("exb")
    turns = (2, 3, 1, 0)
    lower = {dz: 32 * ((exa // 2 + dz) % 4) for dz in turns}
    middle = {dx: 4 * ((exb // 4 + dx) % 4) for dx in turns}
    upper = {dy: (exb + dy) % 4 for dy in turns}
    cores = (16 * (1 - exa % 2), 16 * (exa % 2))
    shifts = [(z, x, y, c) for z in turns for x in turns for y in turns for c in (0, 1)]
    shifts = sorted(shifts, key=lambda t: -sum(min(v, 4 - v) for v in t[:3]))

    def all_others(copy):
        for z, x, y, c in shifts[:-1]:
            copy(lower[z] + cores[c] + (middle[x] + upper[y])).start()

    def wait_bytes(ref, sem):
        pltpu.make_async_copy(ref, ref, sem).wait()

    all_others(part_copy)
    gram_got[pl.ds(device, 1), :] = gram_part[pl.ds(device, 1), :]
    wait_bytes(gram_got.at[pl.ds(0, 127)], sum_sem.at[1])
    gram_row[...] = jnp.sum(gram_got[...], axis=0, keepdims=True) * (1.0 / 65536.0)
    all_others(sum_copy)
    gram[pl.ds(device, 1), :] = gram_row[...]
    all_others(row_copy)
    received[pl.ds(pl.multiple_of(8 * group, 8), 8), :] = outgoing[
        pl.ds(pl.multiple_of(8 * device, 8), 8), :
    ]

    def take_rows(panel):
        if panel == 4:
            wait_bytes(received.at[pl.ds(0, 1016)], row_sem.at[1])
        if panel >= 4:
            for j in range(128 * panel - 512, 128 * panel - 384):
                row = jnp.clip(take[j // 128, j % 128], 0, 1023)
                sketch[j : j + 1, :] = received[pl.ds(row, 1), :]

    wait_bytes(gram.at[pl.ds(0, 127)], sum_sem.at[3])
    factor(gram[...], upper_ref, inverse, work, take_rows)

    for part in range(8):
        core_copy(part).wait_send()
    for part in range(16):
        for stage in range(1, 7):
            link_copy(part, stage).wait_send()
    wait_bytes(outgoing.at[pl.ds(0, 1016)], row_sem.at[0])
    wait_bytes(gram_part.at[pl.ds(0, 127)], sum_sem.at[0])
    wait_bytes(gram_part.at[pl.ds(0, 127)], sum_sem.at[2])


def finish(sketch_ref, inverse_ref, factor_ref, q_ref, upper_ref):
    upper_ref[...] = factor_ref[...]
    q_ref[...] = dot_exact(sketch_ref[...], inverse_ref[...], ((1,), (1,)))


def per_device(features, sign_bits, sample_device, sample_offset):
    f32, i32 = jnp.float32, jnp.int32
    dma = pltpu.SemaphoreType.DMA
    sketch, inverse, upper = pl.pallas_call(
        kernel,
        out_shape=[
            jax.ShapeDtypeStruct((512, 128), f32),
            jax.ShapeDtypeStruct((128, 128), f32),
            jax.ShapeDtypeStruct((128, 128), f32),
        ],
        in_specs=[pl.BlockSpec(memory_space=pltpu.HBM)] * 4,
        out_specs=[pl.BlockSpec(memory_space=pltpu.VMEM)] * 3,
        scratch_shapes=[
            pltpu.VMEM((64, 128), i32),
            pltpu.VMEM((512, 128), i32),
            pltpu.VMEM((512, 128), i32),
            pltpu.VMEM((8192, 128), f32),
            pltpu.VMEM((128, 128), f32),
            pltpu.VMEM((8, 64, 8, 128), f32),
            pltpu.VMEM((8, 64, 8, 128), f32),
            pltpu.VMEM((8, 64, 8, 128), f32),
            pltpu.VMEM((16, 6, 32, 8, 128), f32),
            pltpu.VMEM((16, 2, 32, 8, 128), f32),
            pltpu.VMEM((16, 6, 32, 8, 128), f32),
            pltpu.VMEM((8200, 128), f32),
            pltpu.VMEM((8, 128), i32),
            pltpu.VMEM((8, 128), i32),
            pltpu.SMEM((8, 128), i32),
            pltpu.SMEM((8, 128), i32),
            pltpu.VMEM((1024, 128), f32),
            pltpu.VMEM((1024, 128), f32),
            pltpu.VMEM((128, 128), f32),
            pltpu.VMEM((128, 128), f32),
            pltpu.VMEM((1, 128), f32),
            pltpu.VMEM((128, 128), f32),
            pltpu.VMEM((128, 256), f32),
            dma((11,)),
            dma((2,)),
            dma((8,)),
            dma((8,)),
            dma((16, 6)),
            dma((16, 6)),
            dma((2,)),
            dma((4,)),
        ],
        compiler_params=pltpu.CompilerParams(
            collective_id=0, has_side_effects=True, vmem_limit_bytes=50 * 2**20
        ),
    )(
        features,
        *[pltpu.with_memory_space_constraint(a, pltpu.HBM) for a in (sign_bits.reshape(64, 128), sample_device.reshape(512, 128), sample_offset.reshape(512, 128))],
    )
    return pl.pallas_call(
        finish,
        out_shape=[
            jax.ShapeDtypeStruct((512, 128), f32),
            jax.ShapeDtypeStruct((128, 128), f32),
        ],
        compiler_params=pltpu.CompilerParams(vmem_limit_bytes=8 * 2**20),
    )(sketch, inverse, upper)


def solution(mesh):
    placed = (P(("exa", "exb"), None), P(("exa", "exb")), P(), P())
    return jax.shard_map(
        per_device,
        mesh=mesh,
        in_specs=placed,
        out_specs=(P(("exa", "exb"), None), P()),
        check_vma=False,
    )
```

profile of v0, /device:TPU:1, one launch (start us, length us, event | category | flops | bytes accessed | tf_op | source)
XLA Modules:
  0.0 89.2 jit_solution(14998458548092310485)
XLA Ops:
  0.6 87.5 %shard_map.59 = (f32[512,128]{1,0:T(8,128)S(1)}, f32[128,128]{1,0:T(8,128)S(1)}, f32[128,128]{1,0:T(8,128)S(1)}) custom-call(f32[8192,128]{1,0:T(8,128)} %features_ref.1, s32[64,128]{1,0:T(8,128)} %bitcast.5, s32[512,128]{1,0:T(8,128)} %bitcast.3, s32[512,128]{1,0:T(8,128)} %bitcast.4), custom_call_target="tpu_custom_call" | custom-call | tf_op jit(solution)/shard_map/pallas_call | solution.py:510
  88.1 1.1 %shard_map.60 = (f32[512,128]{1,0:T(8,128)}, f32[128,128]{1,0:T(8,128)}) custom-call(f32[512,128]{1,0:T(8,128)S(1)} %get-tuple-element.5.sketch_ref, f32[128,128]{1,0:T(8,128)S(1)} %get-tuple-element.6.inverse_ref, f32[128,128]{1,0:T(8,128)S(1)} %get-tuple-element.7.factor_ref), custom_call_target="tpu_custom_call" | custom-call | tf_op jit(solution)/shard_map/pallas_call | solution.py:559
where the time goes:
time: 89.3 us; the launch traced here: 89.2 us
  Pallas kernels  88.6 us (99%)
    pallas_call x1, Pallas kernels, per_device(): pl.pallas_call(kernel, out_shape=[jax.ShapeDtypeStruct((512, 128), f32),...  87.5 us

commit v1 on v0

--- a/solution.py
+++ b/solution.py
@@ -9,19 +9,19 @@
 GROUP_BITS = (6, 5, 3, 2, 1, 0)
 STEPS = (96, 32, 12, 4, 3, 1)
 CORE_BIT = 4
-FIRST = (5, 0, 1, 3, 4, 2, 3, 4, 5, 5, 0, 2, 1, 1, 1, 0)
+FIRST = (0, 3, 1, 4, 2, 5, 0, 3, 1, 4, 2, 5, 0, 3, 1, 4)
 ORDER = (
     (0, 0), (1, 0), (2, 0), (3, 0), (4, 0), (5, 0), (6, 0), (7, 0), (0, 1), (1, 1),
-    (2, 1), (3, 1), (4, 1), (5, 1), (8, 1), (10, 1), (12, 1), (6, 1), (7, 1), (11, 1),
-    (9, 1), (15, 1), (13, 1), (5, 2), (3, 2), (2, 2), (4, 2), (0, 2), (14, 1), (11, 2),
-    (6, 2), (12, 2), (7, 2), (8, 2), (1, 2), (2, 3), (5, 3), (13, 2), (3, 3), (9, 2),
-    (10, 2), (12, 3), (11, 3), (14, 2), (6, 3), (4, 3), (15, 2), (13, 3), (2, 4), (1, 3),
-    (5, 4), (7, 3), (0, 3), (14, 3), (12, 4), (10, 3), (11, 4), (3, 4), (8, 3), (1, 4),
-    (13, 4), (15, 3), (2, 5), (6, 4), (9, 3), (10, 4), (14, 4), (0, 4), (12, 5), (5, 5),
-    (4, 4), (15, 4), (1, 5), (8, 4), (13, 5), (11, 5), (7, 4), (0, 5), (10, 5), (9, 4),
-    (14, 5), (2, 6), (3, 5), (8, 5), (15, 5), (4, 5), (1, 6), (12, 6), (6, 5), (9, 5),
-    (0, 6), (7, 5), (10, 6), (13, 6), (5, 6), (4, 6), (8, 6), (3, 6), (15, 6), (14, 6),
-    (11, 6), (7, 6), (9, 6), (6, 6),
+    (2, 1), (3, 1), (4, 1), (5, 1), (6, 1), (7, 1), (8, 1), (9, 1), (10, 1), (11, 1),
+    (12, 1), (13, 1), (14, 1), (15, 1), (2, 2), (3, 2), (5, 2), (4, 2), (0, 2), (1, 2),
+    (8, 2), (9, 2), (11, 2), (10, 2), (6, 2), (7, 2), (14, 2), (15, 2), (3, 3), (2, 3),
+    (12, 2), (13, 2), (0, 3), (1, 3), (9, 3), (8, 3), (5, 3), (4, 3), (6, 3), (7, 3),
+    (15, 3), (14, 3), (11, 3), (10, 3), (12, 3), (13, 3), (1, 4), (0, 4), (3, 4), (2, 4),
+    (5, 4), (4, 4), (7, 4), (6, 4), (9, 4), (8, 4), (11, 4), (10, 4), (13, 4), (12, 4),
+    (15, 4), (14, 4), (3, 5), (2, 5), (4, 5), (5, 5), (1, 5), (0, 5), (9, 5), (8, 5),
+    (10, 5), (11, 5), (7, 5), (6, 5), (15, 5), (14, 5), (2, 6), (3, 6), (13, 5), (12, 5),
+    (1, 6), (0, 6), (8, 6), (9, 6), (4, 6), (5, 6), (7, 6), (6, 6), (14, 6), (15, 6),
+    (10, 6), (11, 6), (13, 6), (12, 6),
 )
 SCALE = 1.0 / 1024.0
 
@@ -326,15 +326,8 @@
             device_id_type=MESH,
         )
 
-    small[1].wait()
-    small[2].wait()
-    sample_tables(group, device, device_ref, offset_ref, give_v, take_v)
     give_copy = pltpu.make_async_copy(give_v, give, table_sem.at[0])
     take_copy = pltpu.make_async_copy(take_v, take, table_sem.at[1])
-    give_copy.start()
-    take_copy.start()
-    give_copy.wait()
-    take_copy.wait()
 
     lines = lax.broadcasted_iota(jnp.int32, (8, 128), 0)
 
@@ -394,7 +387,7 @@
 
         lax.fori_loop(0, 8, body, 0)
 
-    for part, stage in ORDER:
+    for number, (part, stage) in enumerate(ORDER):
         if stage == 0:
             core_copy(part).wait_recv()
             for side in range(2):
@@ -407,13 +400,21 @@
                 link_copy(part, stage + 1).start()
             else:
                 last_stage(part)
+        if number == 7:
+            small[1].wait()
+            small[2].wait()
+            sample_tables(group, device, device_ref, offset_ref, give_v, take_v)
+            give_copy.start()
+            take_copy.start()
     held[8192:8200, :] = jnp.zeros((8, 128), jnp.float32)
+    give_copy.wait()
+    take_copy.wait()
 
     def gather(step, carry):
         for more in range(4):
             to = 4 * step + more
             for k in range(8):
-                row = jnp.clip(give[k, to], 0, 8192)
+                row = give[k, to]
                 outgoing[pl.ds(8 * to + k, 1), :] = held[pl.ds(row, 1), :]
         return carry
 
@@ -479,11 +480,11 @@
     ]
 
     def take_rows(panel):
-        if panel == 4:
+        if panel == 6:
             wait_bytes(received.at[pl.ds(0, 1016)], row_sem.at[1])
-        if panel >= 4:
-            for j in range(128 * panel - 512, 128 * panel - 384):
-                row = jnp.clip(take[j // 128, j % 128], 0, 1023)
+        if panel >= 6:
+            for j in range(256 * (panel - 6), 256 * (panel - 5)):
+                row = take[j // 128, j % 128]
                 sketch[j : j + 1, :] = received[pl.ds(row, 1), :]
 
     wait_bytes(gram.at[pl.ds(0, 127)], sum_sem.at[3])

time: 89.3 us -> 85.8 us (0.961)
  Pallas kernels: 88.6 us -> 85.1 us
    pallas_call x1, Pallas kernels: 87.5 us -> 84 us  [per_device(): pl.pallas_call(kernel, out_shape=[jax.ShapeDtypeStruct((512, 128), f32),...]
where the time goes in v1:
time: 85.8 us; the launch traced here: 85.7 us
  Pallas kernels  85.1 us (99%)
    pallas_call x1, Pallas kernels, per_device(): pl.pallas_call(kernel, out_shape=[jax.ShapeDtypeStruct((512, 128), f32),...  84 us

profile of v1, /device:TPU:1, one launch (start us, length us, event | category | flops | bytes accessed | tf_op | source)
XLA Modules:
  0.0 85.7 jit_solution(13745816601982306522)
XLA Ops:
  0.6 84.0 %shard_map.59 = (f32[512,128]{1,0:T(8,128)S(1)}, f32[128,128]{1,0:T(8,128)S(1)}, f32[128,128]{1,0:T(8,128)S(1)}) custom-call(f32[8192,128]{1,0:T(8,128)} %features_ref.1, s32[64,128]{1,0:T(8,128)} %bitcast.5, s32[512,128]{1,0:T(8,128)} %bitcast.3, s32[512,128]{1,0:T(8,128)} %bitcast.4), custom_call_target="tpu_custom_call" | custom-call | tf_op jit(solution)/shard_map/pallas_call | solution.py:511
  84.6 1.1 %shard_map.60 = (f32[512,128]{1,0:T(8,128)}, f32[128,128]{1,0:T(8,128)}) custom-call(f32[512,128]{1,0:T(8,128)S(1)} %get-tuple-element.5.sketch_ref, f32[128,128]{1,0:T(8,128)S(1)} %get-tuple-element.6.inverse_ref, f32[128,128]{1,0:T(8,128)S(1)} %get-tuple-element.7.factor_ref), custom_call_target="tpu_custom_call" | custom-call | tf_op jit(solution)/shard_map/pallas_call | solution.py:560

commit v2 on v1

--- a/solution.py
+++ b/solution.py
@@ -9,19 +9,19 @@
 GROUP_BITS = (6, 5, 3, 2, 1, 0)
 STEPS = (96, 32, 12, 4, 3, 1)
 CORE_BIT = 4
-FIRST = (0, 3, 1, 4, 2, 5, 0, 3, 1, 4, 2, 5, 0, 3, 1, 4)
+FIRST = (0, 2, 4, 1, 3, 5, 0, 2, 4, 1, 3, 5, 0, 2, 4, 1)
 ORDER = (
     (0, 0), (1, 0), (2, 0), (3, 0), (4, 0), (5, 0), (6, 0), (7, 0), (0, 1), (1, 1),
     (2, 1), (3, 1), (4, 1), (5, 1), (6, 1), (7, 1), (8, 1), (9, 1), (10, 1), (11, 1),
-    (12, 1), (13, 1), (14, 1), (15, 1), (2, 2), (3, 2), (5, 2), (4, 2), (0, 2), (1, 2),
-    (8, 2), (9, 2), (11, 2), (10, 2), (6, 2), (7, 2), (14, 2), (15, 2), (3, 3), (2, 3),
-    (12, 2), (13, 2), (0, 3), (1, 3), (9, 3), (8, 3), (5, 3), (4, 3), (6, 3), (7, 3),
-    (15, 3), (14, 3), (11, 3), (10, 3), (12, 3), (13, 3), (1, 4), (0, 4), (3, 4), (2, 4),
-    (5, 4), (4, 4), (7, 4), (6, 4), (9, 4), (8, 4), (11, 4), (10, 4), (13, 4), (12, 4),
-    (15, 4), (14, 4), (3, 5), (2, 5), (4, 5), (5, 5), (1, 5), (0, 5), (9, 5), (8, 5),
-    (10, 5), (11, 5), (7, 5), (6, 5), (15, 5), (14, 5), (2, 6), (3, 6), (13, 5), (12, 5),
-    (1, 6), (0, 6), (8, 6), (9, 6), (4, 6), (5, 6), (7, 6), (6, 6), (14, 6), (15, 6),
-    (10, 6), (11, 6), (13, 6), (12, 6),
+    (12, 1), (13, 1), (14, 1), (15, 1), (1, 2), (2, 2), (5, 2), (3, 2), (4, 2), (0, 2),
+    (7, 2), (8, 2), (11, 2), (9, 2), (10, 2), (6, 2), (13, 2), (14, 2), (2, 3), (15, 2),
+    (1, 3), (12, 2), (3, 3), (4, 3), (8, 3), (0, 3), (7, 3), (5, 3), (9, 3), (10, 3),
+    (14, 3), (6, 3), (13, 3), (11, 3), (15, 3), (1, 4), (4, 4), (12, 3), (3, 4), (2, 4),
+    (0, 4), (7, 4), (10, 4), (5, 4), (9, 4), (8, 4), (6, 4), (13, 4), (1, 5), (11, 4),
+    (15, 4), (14, 4), (12, 4), (3, 5), (7, 5), (2, 5), (0, 5), (4, 5), (5, 5), (9, 5),
+    (13, 5), (8, 5), (6, 5), (10, 5), (11, 5), (15, 5), (3, 6), (14, 5), (12, 5), (1, 6),
+    (2, 6), (0, 6), (9, 6), (4, 6), (5, 6), (7, 6), (8, 6), (6, 6), (15, 6), (10, 6),
+    (11, 6), (13, 6), (14, 6), (12, 6),
 )
 SCALE = 1.0 / 1024.0
 

time: 85.8 us -> 85.3 us (level)
  no operation moved by 1% of the time
where the time goes in v2:
time: 85.3 us; the launch traced here: 85.2 us
  Pallas kernels  84.6 us (99%)
    pallas_call x1, Pallas kernels, per_device(): pl.pallas_call(kernel, out_shape=[jax.ShapeDtypeStruct((512, 128), f32),...  83.5 us

profile of v2, /device:TPU:1, one launch (start us, length us, event | category | flops | bytes accessed | tf_op | source)
XLA Modules:
  0.0 85.2 jit_solution(9347305844852949959)
XLA Ops:
  0.6 83.5 %shard_map.59 = (f32[512,128]{1,0:T(8,128)S(1)}, f32[128,128]{1,0:T(8,128)S(1)}, f32[128,128]{1,0:T(8,128)S(1)}) custom-call(f32[8192,128]{1,0:T(8,128)} %features_ref.1, s32[64,128]{1,0:T(8,128)} %bitcast.5, s32[512,128]{1,0:T(8,128)} %bitcast.3, s32[512,128]{1,0:T(8,128)} %bitcast.4), custom_call_target="tpu_custom_call" | custom-call | tf_op jit(solution)/shard_map/pallas_call | solution.py:511
  84.1 1.1 %shard_map.60 = (f32[512,128]{1,0:T(8,128)}, f32[128,128]{1,0:T(8,128)}) custom-call(f32[512,128]{1,0:T(8,128)S(1)} %get-tuple-element.5.sketch_ref, f32[128,128]{1,0:T(8,128)S(1)} %get-tuple-element.6.inverse_ref, f32[128,128]{1,0:T(8,128)S(1)} %get-tuple-element.7.factor_ref), custom_call_target="tpu_custom_call" | custom-call | tf_op jit(solution)/shard_map/pallas_call | solution.py:560

commit v3 on v2

--- a/solution.py
+++ b/solution.py
@@ -410,15 +410,15 @@
     give_copy.wait()
     take_copy.wait()
 
-    def gather(step, carry):
-        for more in range(4):
-            to = 4 * step + more
+    for quarter in range(4):
+        for to in range(32 * quarter, 32 * quarter + 32):
             for k in range(8):
-                row = give[k, to]
-                outgoing[pl.ds(8 * to + k, 1), :] = held[pl.ds(row, 1), :]
-        return carry
-
-    lax.fori_loop(0, 32, gather, 0)
+                spot = 8 * to + k
+                outgoing[spot : spot + 1, :] = held[pl.ds(give[k, to], 1), :]
+        some = outgoing[256 * quarter : 256 * quarter + 256, :]
+        more = dot_exact(some, some, ((0,), (0,)))
+        total = more if quarter == 0 else total + more
+    gram_part[...] = total
 
     def row_copy(to):
         return pltpu.make_async_remote_copy(
@@ -429,8 +429,6 @@
             device_id=place_of(to),
             device_id_type=MESH,
         )
-
-    gram_part[...] = dot_exact(outgoing[...], outgoing[...], ((0,), (0,)))
 
     def part_copy(to):
         return pltpu.make_async_remote_copy(

time: 85.3 us -> 84.6 us (level)
  no operation moved by 1% of the time
where the time goes in v3:
time: 84.6 us; the launch traced here: 84.5 us
  Pallas kernels  83.8 us (99%)
    pallas_call x1, Pallas kernels, per_device(): pl.pallas_call(kernel, out_shape=[jax.ShapeDtypeStruct((512, 128), f32),...  82.7 us

profile of v3, /device:TPU:1, one launch (start us, length us, event | category | flops | bytes accessed | tf_op | source)
XLA Modules:
  0.0 84.5 jit_solution(6676529121739491167)
XLA Ops:
  0.6 82.7 %shard_map.59 = (f32[512,128]{1,0:T(8,128)S(1)}, f32[128,128]{1,0:T(8,128)S(1)}, f32[128,128]{1,0:T(8,128)S(1)}) custom-call(f32[8192,128]{1,0:T(8,128)} %features_ref.1, s32[64,128]{1,0:T(8,128)} %bitcast.5, s32[512,128]{1,0:T(8,128)} %bitcast.3, s32[512,128]{1,0:T(8,128)} %bitcast.4), custom_call_target="tpu_custom_call" | custom-call | tf_op jit(solution)/shard_map/pallas_call | solution.py:509
  83.4 1.1 %shard_map.60 = (f32[512,128]{1,0:T(8,128)}, f32[128,128]{1,0:T(8,128)}) custom-call(f32[512,128]{1,0:T(8,128)S(1)} %get-tuple-element.5.sketch_ref, f32[128,128]{1,0:T(8,128)S(1)} %get-tuple-element.6.inverse_ref, f32[128,128]{1,0:T(8,128)S(1)} %get-tuple-element.7.factor_ref), custom_call_target="tpu_custom_call" | custom-call | tf_op jit(solution)/shard_map/pallas_call | solution.py:558

commit v4 on v3

--- a/solution.py
+++ b/solution.py
@@ -361,8 +361,8 @@
             return a + b, sign * (a - b)
 
         def body(step, carry):
-            for more in range(4):
-                i = 4 * step + more
+            for more in range(8):
+                i = 8 * step + more
                 for side, (a, b) in enumerate(zip(pair(i), pair(i + 16))):
                     if stage == 2:
                         a, b = sublane_hadamard(a, lines), sublane_hadamard(b, lines)
@@ -371,7 +371,7 @@
                     send[part, stage, 2 * i + side] = a - b
             return carry
 
-        lax.fori_loop(0, 4, body, 0)
+        lax.fori_loop(0, 2, body, 0)
 
     def last_stage(part):
         sign = link_sign[(FIRST[part] + 5) % 6] * SCALE

time: 84.6 us -> 84.6 us (level)
  no operation moved by 1% of the time
where the time goes in v4:
time: 84.6 us; the launch traced here: 84.4 us
  Pallas kernels  83.8 us (99%)
    pallas_call x1, Pallas kernels, per_device(): pl.pallas_call(kernel, out_shape=[jax.ShapeDtypeStruct((512, 128), f32),...  82.7 us

profile of v4, /device:TPU:1, one launch (start us, length us, event | category | flops | bytes accessed | tf_op | source)
XLA Modules:
  0.0 84.4 jit_solution(11408101871775457337)
XLA Ops:
  0.6 82.7 %shard_map.59 = (f32[512,128]{1,0:T(8,128)S(1)}, f32[128,128]{1,0:T(8,128)S(1)}, f32[128,128]{1,0:T(8,128)S(1)}) custom-call(f32[8192,128]{1,0:T(8,128)} %features_ref.1, s32[64,128]{1,0:T(8,128)} %bitcast.5, s32[512,128]{1,0:T(8,128)} %bitcast.3, s32[512,128]{1,0:T(8,128)} %bitcast.4), custom_call_target="tpu_custom_call" | custom-call | tf_op jit(solution)/shard_map/pallas_call | solution.py:509
  83.4 1.1 %shard_map.60 = (f32[512,128]{1,0:T(8,128)}, f32[128,128]{1,0:T(8,128)}) custom-call(f32[512,128]{1,0:T(8,128)S(1)} %get-tuple-element.5.sketch_ref, f32[128,128]{1,0:T(8,128)S(1)} %get-tuple-element.6.inverse_ref, f32[128,128]{1,0:T(8,128)S(1)} %get-tuple-element.7.factor_ref), custom_call_target="tpu_custom_call" | custom-call | tf_op jit(solution)/shard_map/pallas_call | solution.py:558
